TPU v7x, 128 devices: a whole 4x4x4 slice. The times are simulated.
128 devices in a mesh: tm: 16 (over z, x), pack: 8 (over y, core).
Axes of the slice: x: 4, y: 4, z: 4, core: 2. Of those that a mesh axis runs over, the one named last changes fastest.
Arguments:
- queries: bfloat16 [8, 8192, 1024], P('pack', 'tm'), may hold values from -8 to 8
- keys: bfloat16 [8, 8192, 1024], P('pack', 'tm'), may hold values from -8 to 8
- values: bfloat16 [8, 8192, 1024], P('pack', 'tm'), may hold values from -6 to 6
- w_out: bfloat16 [1024, 1024], replicated, may hold values from -0.1875 to 0.1875
- norm_gain: float32 [1024], replicated, may hold values from 0.1 to 1.9
- block_owner: int32 [8, 64, 1], P('pack', 'tm'), may hold values from 0 to 7; in each aligned block of 4 rows (0 to 3, 4 to 7, ..., all dimensions but the last counted through in order) at most 2 rows name the same one
- block_base: int32 [8, 64], P('pack', 'tm'), may hold values from 0 to 112
- frame_offset: int32 [8, 64, 128], P('pack', 'tm'), may hold values from 0 to 15, never falling along the last dimension, each value on 1 to 16 neighbouring positions
Outputs:
- encoded: bfloat16 [8, 8192, 1024], P('pack', 'tm')
- pooled: bfloat16 [8, 2048, 1024], P('pack', 'tm')
Inputs may be any that keep to these rules, and one draw needn't show every extreme that they name: `block_owner`: among the 4 blocks of one device (aligned runs of the list), at most 2 name the same owner. `frame_offset`: within each block of 128 frames the offsets never fall and each of 0 to 15 occurs.
All inputs are finite; a program needn't handle non-finite values.
Results may differ from a plain program's by a relative error of at most 0.008.
Values may be sent and summed in bfloat16 or wider, within the bound.
A program may use at most 128 MiB of HBM per device.

v0:
```python
import jax
import jax.numpy as jnp
from jax import lax
from jax.sharding import PartitionSpec as P

HEADS = 16
LANDMARKS = 256
BLOCK = 128
POOL_DEV = 128


def mix_heads(query_rows, mark_keys, mark_values, head_count):
    row_count, model_width = query_rows.shape
    head_dim = model_width // head_count
    query_heads = query_rows.reshape(row_count, head_count, head_dim)
    key_heads = mark_keys.reshape(-1, head_count, head_dim)
    value_heads = mark_values.reshape(-1, head_count, head_dim)
    scores = jnp.einsum(
        "nhe,mhe->nhm", query_heads, key_heads, preferred_element_type=jnp.float32
    ) * head_dim ** (-0.5)
    weights = jnp.exp(scores - jnp.max(scores, axis=-1, keepdims=True))
    totals = jnp.sum(weights, axis=-1)
    blended = jnp.einsum(
        "nhm,mhe->nhe",
        weights.astype(jnp.bfloat16),
        value_heads,
        preferred_element_type=jnp.float32,
    )
    return (blended / totals[..., None]).reshape(row_count, model_width).astype(jnp.bfloat16)


def local(queries, keys, values, w_out, norm_gain, block_owner, block_base, frame_offset):
    frame_q = queries[0]
    frame_k = keys[0]
    frame_v = values[0]
    frame_count, model_width = frame_q.shape
    span = frame_count // LANDMARKS
    mark_queries = jnp.mean(
        frame_q.reshape(LANDMARKS, span, model_width), axis=1, dtype=jnp.float32
    ).astype(jnp.bfloat16)
    mark_keys = jnp.mean(
        frame_k.reshape(LANDMARKS, span, model_width), axis=1, dtype=jnp.float32
    ).astype(jnp.bfloat16)
    mark_values = mix_heads(mark_queries, frame_k, frame_v, HEADS)
    head_dim = model_width // HEADS
    query_heads = frame_q.reshape(frame_count, HEADS, head_dim)

    def absorb(running, piece_keys, piece_values):
        running_top, running_sum, running_acc = running
        key_heads = piece_keys.reshape(-1, HEADS, head_dim)
        value_heads = piece_values.reshape(-1, HEADS, head_dim)
        scores = jnp.einsum(
            "nhe,mhe->nhm", query_heads, key_heads, preferred_element_type=jnp.float32
        ) * head_dim ** (-0.5)
        new_top = jnp.maximum(running_top, jnp.max(scores, axis=-1))
        weights = jnp.exp(scores - new_top[..., None])
        rescale = jnp.exp(running_top - new_top)
        running_sum = running_sum * rescale + jnp.sum(weights, axis=-1)
        running_acc = running_acc * rescale[..., None] + jnp.einsum(
            "nhm,mhe->nhe",
            weights.astype(jnp.bfloat16),
            value_heads,
            preferred_element_type=jnp.float32,
        )
        return (new_top, running_sum, running_acc)

    start_state = (
        jnp.full((frame_count, HEADS), -1e30, jnp.float32),
        jnp.zeros((frame_count, HEADS), jnp.float32),
        jnp.zeros((frame_count, HEADS, head_dim), jnp.float32),
    )
    running = start_state
    piece_keys = lax.all_gather(mark_keys, "tm", axis=0, tiled=True)
    piece_values = lax.all_gather(mark_values, "tm", axis=0, tiled=True)
    stacked = (
        piece_keys.reshape(-1, LANDMARKS, model_width),
        piece_values.reshape(-1, LANDMARKS, model_width),
    )

    def advance(inner_state, sub_block):
        return (absorb(inner_state, sub_block[0], sub_block[1]), None)

    running, unused = lax.scan(advance, running, stacked)
    final_top, final_sum, final_acc = running
    attended = (
        (final_acc / final_sum[..., None]).reshape(frame_count, model_width).astype(jnp.bfloat16)
    )
    projected = jnp.dot(attended, w_out, preferred_element_type=jnp.float32)
    scaled = projected * lax.rsqrt(jnp.mean(projected * projected, axis=-1, keepdims=True) + 1e-06)
    encoded = (scaled * norm_gain).astype(jnp.bfloat16)
    pack_count = lax.axis_size("pack")
    owners = block_owner[0, :, 0]
    block_count = owners.shape[0]
    slot_count = max(2, 2 * block_count // pack_count)
    pack_range = jnp.arange(pack_count, dtype=jnp.int32)
    dest_hits = (owners[:, None] == pack_range[None, :]).astype(jnp.int32)
    slot_rank = jnp.sum((jnp.cumsum(dest_hits, axis=0) - dest_hits) * dest_hits, axis=1)
    chosen = (owners[None, None, :] == pack_range[:, None, None]) & (
        slot_rank[None, None, :] == jnp.arange(slot_count, dtype=jnp.int32)[None, :, None]
    )
    filled = jnp.any(chosen, axis=-1)
    source_block = jnp.sum(
        chosen.astype(jnp.int32) * jnp.arange(block_count, dtype=jnp.int32)[None, None, :], axis=-1
    )
    frame_blocks = encoded.reshape(block_count, BLOCK, model_width)
    offsets = frame_offset[0]
    block_bases = block_base[0]
    sent_rows = jnp.where(
        filled[..., None, None],
        jnp.take(frame_blocks, source_block, axis=0),
        jnp.zeros((), jnp.bfloat16),
    )
    row_targets = jnp.take(block_bases, source_block)[..., None] + jnp.take(
        offsets, source_block, axis=0
    )
    sent_targets = jnp.where(filled[..., None], row_targets, -1).astype(jnp.bfloat16)
    got_rows, got_targets = (
        lax.all_to_all(sent_rows, "pack", split_axis=0, concat_axis=0, tiled=True),
        lax.all_to_all(sent_targets, "pack", split_axis=0, concat_axis=0, tiled=True),
    )
    pool_rows = jnp.arange(POOL_DEV, dtype=jnp.int32).astype(jnp.bfloat16)
    placing = got_targets[:, :, None, :] == pool_rows[None, None, :, None]
    pool_sums = jnp.einsum(
        "scrf,scfd->rd", placing.astype(jnp.bfloat16), got_rows, preferred_element_type=jnp.float32
    )
    pool_counts = jnp.sum(placing.astype(jnp.float32), axis=(0, 1, 3))
    pooled = (pool_sums / jnp.maximum(pool_counts, 1.0)[:, None]).astype(jnp.bfloat16)
    return (encoded[None], pooled[None])


def solution(mesh):
    return jax.shard_map(
        local,
        mesh=mesh,
        in_specs=(
            P("pack", "tm", None),
            P("pack", "tm", None),
            P("pack", "tm", None),
            P(),
            P(),
            P("pack", "tm", None),
            P("pack", "tm"),
            P("pack", "tm", None),
        ),
        out_specs=(P("pack", "tm", None), P("pack", "tm", None)),
        check_vma=False,
    )
```

profile of v0, /device:TPU:1, one launch (start us, length us, event | category | flops | bytes accessed | tf_op | source)
XLA Modules:
  0.0 595.5 jit_solution(14726853507628708703)
XLA Ops:
  7.2 3.6 reshape.138
  10.8 5.1 reduce_sum.75
  23.6 2.8 bitcast_reduce_fusion.1
  28.4 2.7 divide_convert_fusion.1
  33.2 2.3 reshape.137
  35.5 5.1 reduce_sum.74
  45.9 6.0 %all-to-all-start = ((bf16[8,2,128]{2,1,0:T(2,128)(2,1)}), bf16[8,2,128]{2,1,0:T(2,128)(2,1)S(1)}, u32[]{:S(2)}, u32[]{:S(2)}) async-start(bf16[8,2,128]{2,1,0:T(2,128)(2,1)} %select_convert_fusion), calls=%async_computation | async-start | bytes 8192 | tf_op jit(solution)/shard_map/all_to_all | solution.py:119
  53.2 54.2 %all-gather.5.cloned.1.call-done = bf16[4096,1024]{1,0:T(8,128)(2,1)} async-done(((bf16[256,1024]{1,0:T(8,128)(2,1)}), bf16[4096,1024]{1,0:T(8,128)(2,1)}) %all-gather.5.cloned.1.call-update) | async-done | bytes 8388624 | tf_op jit(solution)/shard_map/all_gather | solution.py:74
  107.4 72.6 %all-gather.3.cloned.1.call-done = bf16[4096,1024]{1,0:T(8,128)(2,1)} async-done(((bf16[256,1024]{1,0:T(8,128)(2,1)}), bf16[4096,1024]{1,0:T(8,128)(2,1)}) %all-gather.3.cloned.1.call-update) | async-done | bytes 8388624 | tf_op jit(solution)/shard_map/all_gather | solution.py:73
  180.1 338.5 %while.15 = (s32[]{:T(128)}, f32[512,16]{0,1:T(8,128)S(1)}, f32[512,16]{0,1:T(8,128)S(1)}, f32[512,16,64]{0,2,1:T(8,128)}, bf16[16,256,1024]{2,1,0:T(8,128)(2,1)...) while((s32[]{:T(128)}, f32[512,16]{0,1:T(8,128)S(1)}, ...), condition=%wide.region_7.8_spmd.clone, body=%wide.region_4.7_spmd.clone.sunk | while | flops 555261952 | bytes 36175980 | solution.py:83
  183.4 5.8 bitcast_reduce_fusion.3
  189.1 4.8 fusion.71
  194.2 6.5 %bitcast_add_fusion.2 = f32[512,16,64]{0,2,1:T(8,128)} fusion(f32[512,16,64]{0,2,1:T(8,128)} %get-tuple-element.187, bf16[256,16,64]{0,2,1:T(8,128)(2,1)S(1)} %bitcast.93, f32[16,256,512]{2,1,0:T(8,128)} %get-tuple-element.171, f32[512,16]{0,1:T(8,128)S(1)} %select_maximum_fusion.2, f32[512,16]{0,1:T(8,128)S(1)} %get-tuple-element.174, pred[]{:T(512)S(6)} %compare.3), kind=kOutput, calls=%fused_computation.11.clone.1 | convolution fusion | flops 276299776 | bytes 13172737 | tf_op jit(solution)/shard_map/while/body/eval_jaxpr/nhm,mhe->nhe/dot_general | solution.py:59
  204.0 5.8 bitcast_reduce_fusion.3
  209.7 4.8 fusion.71
  214.8 7.1 %bitcast_add_fusion.2 = f32[512,16,64]{0,2,1:T(8,128)} fusion(f32[512,16,64]{0,2,1:T(8,128)} %get-tuple-element.187, bf16[256,16,64]{0,2,1:T(8,128)(2,1)S(1)} %bitcast.93, f32[16,256,512]{2,1,0:T(8,128)} %get-tuple-element.171, f32[512,16]{0,1:T(8,128)S(1)} %select_maximum_fusion.2, f32[512,16]{0,1:T(8,128)S(1)} %get-tuple-element.174, pred[]{:T(512)S(6)} %compare.3), kind=kOutput, calls=%fused_computation.11.clone.1 | convolution fusion | flops 276299776 | bytes 13172737 | tf_op jit(solution)/shard_map/while/body/eval_jaxpr/nhm,mhe->nhe/dot_general | solution.py:59
  225.2 5.8 bitcast_reduce_fusion.3
  230.9 4.8 fusion.71
  236.0 7.1 %bitcast_add_fusion.2 = f32[512,16,64]{0,2,1:T(8,128)} fusion(f32[512,16,64]{0,2,1:T(8,128)} %get-tuple-element.187, bf16[256,16,64]{0,2,1:T(8,128)(2,1)S(1)} %bitcast.93, f32[16,256,512]{2,1,0:T(8,128)} %get-tuple-element.171, f32[512,16]{0,1:T(8,128)S(1)} %select_maximum_fusion.2, f32[512,16]{0,1:T(8,128)S(1)} %get-tuple-element.174, pred[]{:T(512)S(6)} %compare.3), kind=kOutput, calls=%fused_computation.11.clone.1 | convolution fusion | flops 276299776 | bytes 13172737 | tf_op jit(solution)/shard_map/while/body/eval_jaxpr/nhm,mhe->nhe/dot_general | solution.py:59
  246.4 5.8 bitcast_reduce_fusion.3
  252.1 4.8 fusion.71
  257.2 7.1 %bitcast_add_fusion.2 = f32[512,16,64]{0,2,1:T(8,128)} fusion(f32[512,16,64]{0,2,1:T(8,128)} %get-tuple-element.187, bf16[256,16,64]{0,2,1:T(8,128)(2,1)S(1)} %bitcast.93, f32[16,256,512]{2,1,0:T(8,128)} %get-tuple-element.171, f32[512,16]{0,1:T(8,128)S(1)} %select_maximum_fusion.2, f32[512,16]{0,1:T(8,128)S(1)} %get-tuple-element.174, pred[]{:T(512)S(6)} %compare.3), kind=kOutput, calls=%fused_computation.11.clone.1 | convolution fusion | flops 276299776 | bytes 13172737 | tf_op jit(solution)/shard_map/while/body/eval_jaxpr/nhm,mhe->nhe/dot_general | solution.py:59
  267.6 5.8 bitcast_reduce_fusion.3
  273.3 4.8 fusion.71
  278.4 7.1 %bitcast_add_fusion.2 = f32[512,16,64]{0,2,1:T(8,128)} fusion(f32[512,16,64]{0,2,1:T(8,128)} %get-tuple-element.187, bf16[256,16,64]{0,2,1:T(8,128)(2,1)S(1)} %bitcast.93, f32[16,256,512]{2,1,0:T(8,128)} %get-tuple-element.171, f32[512,16]{0,1:T(8,128)S(1)} %select_maximum_fusion.2, f32[512,16]{0,1:T(8,128)S(1)} %get-tuple-element.174, pred[]{:T(512)S(6)} %compare.3), kind=kOutput, calls=%fused_computation.11.clone.1 | convolution fusion | flops 276299776 | bytes 13172737 | tf_op jit(solution)/shard_map/while/body/eval_jaxpr/nhm,mhe->nhe/dot_general | solution.py:59
  288.8 5.8 bitcast_reduce_fusion.3
  294.5 4.8 fusion.71
  299.6 7.1 %bitcast_add_fusion.2 = f32[512,16,64]{0,2,1:T(8,128)} fusion(f32[512,16,64]{0,2,1:T(8,128)} %get-tuple-element.187, bf16[256,16,64]{0,2,1:T(8,128)(2,1)S(1)} %bitcast.93, f32[16,256,512]{2,1,0:T(8,128)} %get-tuple-element.171, f32[512,16]{0,1:T(8,128)S(1)} %select_maximum_fusion.2, f32[512,16]{0,1:T(8,128)S(1)} %get-tuple-element.174, pred[]{:T(512)S(6)} %compare.3), kind=kOutput, calls=%fused_computation.11.clone.1 | convolution fusion | flops 276299776 | bytes 13172737 | tf_op jit(solution)/shard_map/while/body/eval_jaxpr/nhm,mhe->nhe/dot_general | solution.py:59
  309.9 5.8 bitcast_reduce_fusion.3
  315.7 4.8 fusion.71
  320.8 7.1 %bitcast_add_fusion.2 = f32[512,16,64]{0,2,1:T(8,128)} fusion(f32[512,16,64]{0,2,1:T(8,128)} %get-tuple-element.187, bf16[256,16,64]{0,2,1:T(8,128)(2,1)S(1)} %bitcast.93, f32[16,256,512]{2,1,0:T(8,128)} %get-tuple-element.171, f32[512,16]{0,1:T(8,128)S(1)} %select_maximum_fusion.2, f32[512,16]{0,1:T(8,128)S(1)} %get-tuple-element.174, pred[]{:T(512)S(6)} %compare.3), kind=kOutput, calls=%fused_computation.11.clone.1 | convolution fusion | flops 276299776 | bytes 13172737 | tf_op jit(solution)/shard_map/while/body/eval_jaxpr/nhm,mhe->nhe/dot_general | solution.py:59
  331.1 5.8 bitcast_reduce_fusion.3
  336.9 4.8 fusion.71
  342.0 7.1 %bitcast_add_fusion.2 = f32[512,16,64]{0,2,1:T(8,128)} fusion(f32[512,16,64]{0,2,1:T(8,128)} %get-tuple-element.187, bf16[256,16,64]{0,2,1:T(8,128)(2,1)S(1)} %bitcast.93, f32[16,256,512]{2,1,0:T(8,128)} %get-tuple-element.171, f32[512,16]{0,1:T(8,128)S(1)} %select_maximum_fusion.2, f32[512,16]{0,1:T(8,128)S(1)} %get-tuple-element.174, pred[]{:T(512)S(6)} %compare.3), kind=kOutput, calls=%fused_computation.11.clone.1 | convolution fusion | flops 276299776 | bytes 13172737 | tf_op jit(solution)/shard_map/while/body/eval_jaxpr/nhm,mhe->nhe/dot_general | solution.py:59
  352.3 5.8 bitcast_reduce_fusion.3
  358.1 4.8 fusion.71
  363.2 7.1 %bitcast_add_fusion.2 = f32[512,16,64]{0,2,1:T(8,128)} fusion(f32[512,16,64]{0,2,1:T(8,128)} %get-tuple-element.187, bf16[256,16,64]{0,2,1:T(8,128)(2,1)S(1)} %bitcast.93, f32[16,256,512]{2,1,0:T(8,128)} %get-tuple-element.171, f32[512,16]{0,1:T(8,128)S(1)} %select_maximum_fusion.2, f32[512,16]{0,1:T(8,128)S(1)} %get-tuple-element.174, pred[]{:T(512)S(6)} %compare.3), kind=kOutput, calls=%fused_computation.11.clone.1 | convolution fusion | flops 276299776 | bytes 13172737 | tf_op jit(solution)/shard_map/while/body/eval_jaxpr/nhm,mhe->nhe/dot_general | solution.py:59
  373.5 5.8 bitcast_reduce_fusion.3
  379.3 4.8 fusion.71
  384.4 7.1 %bitcast_add_fusion.2 = f32[512,16,64]{0,2,1:T(8,128)} fusion(f32[512,16,64]{0,2,1:T(8,128)} %get-tuple-element.187, bf16[256,16,64]{0,2,1:T(8,128)(2,1)S(1)} %bitcast.93, f32[16,256,512]{2,1,0:T(8,128)} %get-tuple-element.171, f32[512,16]{0,1:T(8,128)S(1)} %select_maximum_fusion.2, f32[512,16]{0,1:T(8,128)S(1)} %get-tuple-element.174, pred[]{:T(512)S(6)} %compare.3), kind=kOutput, calls=%fused_computation.11.clone.1 | convolution fusion | flops 276299776 | bytes 13172737 | tf_op jit(solution)/shard_map/while/body/eval_jaxpr/nhm,mhe->nhe/dot_general | solution.py:59
  394.7 5.8 bitcast_reduce_fusion.3
  400.5 4.8 fusion.71
  405.5 7.1 %bitcast_add_fusion.2 = f32[512,16,64]{0,2,1:T(8,128)} fusion(f32[512,16,64]{0,2,1:T(8,128)} %get-tuple-element.187, bf16[256,16,64]{0,2,1:T(8,128)(2,1)S(1)} %bitcast.93, f32[16,256,512]{2,1,0:T(8,128)} %get-tuple-element.171, f32[512,16]{0,1:T(8,128)S(1)} %select_maximum_fusion.2, f32[512,16]{0,1:T(8,128)S(1)} %get-tuple-element.174, pred[]{:T(512)S(6)} %compare.3), kind=kOutput, calls=%fused_computation.11.clone.1 | convolution fusion | flops 276299776 | bytes 13172737 | tf_op jit(solution)/shard_map/while/body/eval_jaxpr/nhm,mhe->nhe/dot_general | solution.py:59
  415.9 5.8 bitcast_reduce_fusion.3
  421.7 4.8 fusion.71
  426.7 7.1 %bitcast_add_fusion.2 = f32[512,16,64]{0,2,1:T(8,128)} fusion(f32[512,16,64]{0,2,1:T(8,128)} %get-tuple-element.187, bf16[256,16,64]{0,2,1:T(8,128)(2,1)S(1)} %bitcast.93, f32[16,256,512]{2,1,0:T(8,128)} %get-tuple-element.171, f32[512,16]{0,1:T(8,128)S(1)} %select_maximum_fusion.2, f32[512,16]{0,1:T(8,128)S(1)} %get-tuple-element.174, pred[]{:T(512)S(6)} %compare.3), kind=kOutput, calls=%fused_computation.11.clone.1 | convolution fusion | flops 276299776 | bytes 13172737 | tf_op jit(solution)/shard_map/while/body/eval_jaxpr/nhm,mhe->nhe/dot_general | solution.py:59
  437.1 5.8 bitcast_reduce_fusion.3
  442.9 4.8 fusion.71
  447.9 7.1 %bitcast_add_fusion.2 = f32[512,16,64]{0,2,1:T(8,128)} fusion(f32[512,16,64]{0,2,1:T(8,128)} %get-tuple-element.187, bf16[256,16,64]{0,2,1:T(8,128)(2,1)S(1)} %bitcast.93, f32[16,256,512]{2,1,0:T(8,128)} %get-tuple-element.171, f32[512,16]{0,1:T(8,128)S(1)} %select_maximum_fusion.2, f32[512,16]{0,1:T(8,128)S(1)} %get-tuple-element.174, pred[]{:T(512)S(6)} %compare.3), kind=kOutput, calls=%fused_computation.11.clone.1 | convolution fusion | flops 276299776 | bytes 13172737 | tf_op jit(solution)/shard_map/while/body/eval_jaxpr/nhm,mhe->nhe/dot_general | solution.py:59
  458.3 5.8 bitcast_reduce_fusion.3
  464.1 4.8 fusion.71
  469.1 7.1 %bitcast_add_fusion.2 = f32[512,16,64]{0,2,1:T(8,128)} fusion(f32[512,16,64]{0,2,1:T(8,128)} %get-tuple-element.187, bf16[256,16,64]{0,2,1:T(8,128)(2,1)S(1)} %bitcast.93, f32[16,256,512]{2,1,0:T(8,128)} %get-tuple-element.171, f32[512,16]{0,1:T(8,128)S(1)} %select_maximum_fusion.2, f32[512,16]{0,1:T(8,128)S(1)} %get-tuple-element.174, pred[]{:T(512)S(6)} %compare.3), kind=kOutput, calls=%fused_computation.11.clone.1 | convolution fusion | flops 276299776 | bytes 13172737 | tf_op jit(solution)/shard_map/while/body/eval_jaxpr/nhm,mhe->nhe/dot_general | solution.py:59
  479.5 5.8 bitcast_reduce_fusion.3
  485.3 4.8 fusion.71
  490.3 7.1 %bitcast_add_fusion.2 = f32[512,16,64]{0,2,1:T(8,128)} fusion(f32[512,16,64]{0,2,1:T(8,128)} %get-tuple-element.187, bf16[256,16,64]{0,2,1:T(8,128)(2,1)S(1)} %bitcast.93, f32[16,256,512]{2,1,0:T(8,128)} %get-tuple-element.171, f32[512,16]{0,1:T(8,128)S(1)} %select_maximum_fusion.2, f32[512,16]{0,1:T(8,128)S(1)} %get-tuple-element.174, pred[]{:T(512)S(6)} %compare.3), kind=kOutput, calls=%fused_computation.11.clone.1 | convolution fusion | flops 276299776 | bytes 13172737 | tf_op jit(solution)/shard_map/while/body/eval_jaxpr/nhm,mhe->nhe/dot_general | solution.py:59
  500.7 5.8 bitcast_reduce_fusion.3
  506.5 4.8 fusion.71
  511.5 7.1 %bitcast_add_fusion.2 = f32[512,16,64]{0,2,1:T(8,128)} fusion(f32[512,16,64]{0,2,1:T(8,128)} %get-tuple-element.187, bf16[256,16,64]{0,2,1:T(8,128)(2,1)S(1)} %bitcast.93, f32[16,256,512]{2,1,0:T(8,128)} %get-tuple-element.171, f32[512,16]{0,1:T(8,128)S(1)} %select_maximum_fusion.2, f32[512,16]{0,1:T(8,128)S(1)} %get-tuple-element.174, pred[]{:T(512)S(6)} %compare.3), kind=kOutput, calls=%fused_computation.11.clone.1 | convolution fusion | flops 276299776 | bytes 13172737 | tf_op jit(solution)/shard_map/while/body/eval_jaxpr/nhm,mhe->nhe/dot_general | solution.py:59
  523.5 2.8 gather_fusion.2
  526.3 4.6 select_select_fusion
  531.0 5.1 all-to-all-start.1
  536.3 2.8 fusion.60
  539.2 45.8 %all-to-all-done.1 = bf16[8,2,128,1024]{3,2,1,0:T(8,128)(2,1)} async-done(((bf16[8,2,128,1024]{3,2,1,0:T(8,128)(2,1)}), bf16[8,2,128,1024]{3,2,1,0:T(8,128)(2,1)}, u32[]{:S(2)}, u32[]{:S(2)}) %all-to-all-start.1) | async-done | bytes 4194336 | tf_op jit(solution)/shard_map/all_to_all | solution.py:118
  585.0 3.7 fusion.40
  (158 shorter events, 80.2 us)
Async XLA Ops:
  7.2 513.3 %copy-start = (bf16[1024,1024]{1,0:T(8,128)(2,1)S(1)}, bf16[1024,1024]{1,0:T(8,128)(2,1)}, u32[]{:S(2)}) copy-start(bf16[1024,1024]{1,0:T(8,128)(2,1)} %param.13) | copy-start | bytes 6291460
  7.2 12.9 %copy-start.3 = (bf16[1,512,1024]{2,1,0:T(8,128)(2,1)S(1)}, bf16[1,512,1024]{2,1,0:T(8,128)(2,1)}, u32[]{:S(2)}) copy-start(bf16[1,512,1024]{2,1,0:T(8,128)(2,1)} %param.11) | copy-start | bytes 3145732
  7.2 100.3 %all-gather.5.cloned.1.call-start = ((), (), s32[]{:S(2)}) async-start(), calls=%async_computation.3 | async-start | bytes 8912896 | tf_op jit(solution)/shard_map/all_gather | solution.py:74
  26.4 1.9 copy-start.6
  33.1 9.7 %copy-start.8 = (s32[1,4,1]{1,2,0:T(1,128)S(1)}, s32[1,4,1]{1,2,0:T(1,128)}, u32[]{:S(2)}) copy-start(s32[1,4,1]{1,2,0:T(1,128)} %param.15) | copy-start | bytes 52
  33.1 10.3 %copy-start.1 = (s32[1,4]{1,0:T(1,128)S(1)}, s32[1,4]{1,0:T(1,128)}, u32[]{:S(2)}) copy-start(s32[1,4]{1,0:T(1,128)} %param.16) | copy-start | bytes 52
  33.1 146.9 %all-gather.3.cloned.1.call-start = ((), (), s32[]{:S(2)}) async-start(), calls=%async_computation.2 | async-start | bytes 8912896 | tf_op jit(solution)/shard_map/all_gather | solution.py:73
  35.5 9.2 %copy-start.5 = (s32[1,4,128]{2,1,0:T(4,128)S(1)}, s32[1,4,128]{2,1,0:T(4,128)}, u32[]{:S(2)}) copy-start(s32[1,4,128]{2,1,0:T(4,128)} %param.17) | copy-start | bytes 6148
  35.5 16.4 %copy-start.4 = (bf16[1,512,1024]{2,1,0:T(8,128)(2,1)S(1)}, bf16[1,512,1024]{2,1,0:T(8,128)(2,1)}, u32[]{:S(2)}) copy-start(bf16[1,512,1024]{2,1,0:T(8,128)(2,1)} %param.10) | copy-start | bytes 3145732
  45.9 485.1 %all-to-all-start = ((bf16[8,2,128]{2,1,0:T(2,128)(2,1)}), bf16[8,2,128]{2,1,0:T(2,128)(2,1)S(1)}, u32[]{:S(2)}, u32[]{:S(2)}) async-start(bf16[8,2,128]{2,1,0:T(2,128)(2,1)} %select_convert_fusion), calls=%async_computation | async-start | bytes 8192 | tf_op jit(solution)/shard_map/all_to_all | solution.py:119
  518.6 4.7 copy-start.7
  521.9 1.4 copy-start.2
  531.0 54.0 %all-to-all-start.1 = ((bf16[8,2,128,1024]{3,2,1,0:T(8,128)(2,1)}), bf16[8,2,128,1024]{3,2,1,0:T(8,128)(2,1)}, u32[]{:S(2)}, u32[]{:S(2)}) async-start(bf16[8,2,128,1024]{3,2,1,0:T(8,128)(2,1)} %select_select_fusion), calls=%async_computation.1 | async-start | bytes 8388608 | tf_op jit(solution)/shard_map/all_to_all | solution.py:118
Sparse Core Ops, SparseCore 0:
  33.2 74.1 all-gather.4
  109.6 70.4 all-gather.2
where the time goes:
time: 599 us; the launch traced here: 596 us
  matrix products  215 us (36%)
  waiting for transfers between devices  173 us (29%)
  other arithmetic  105 us (18%)
  local copies, waits for them, and re-layouts  77.1 us (13%)
  between operations  14.2 us (2%)
  starting transfers between devices  11.1 us (2%)
    dot_general x16, matrix products, absorb(): jnp.einsum('nhm,mhe->nhe', weights.astype(jnp.bfloat16), value_heads, pre...  113 us
    dot_general x16, matrix products, absorb(): jnp.einsum('nhe,mhe->nhm', query_heads, key_heads, preferred_element_type...  92 us
    reduce_sum x16, other arithmetic, absorb(): running_sum = running_sum * rescale + jnp.sum(weights, axis=-1)  77.1 us
    all_gather x1, waiting for transfers between devices, local(): piece_keys = lax.all_gather(mark_keys, 'tm', axis=0, tiled=True)  72.6 us
    dynamic_slice x48, local copies, waits for them, and re-layouts, local(): running, unused = lax.scan(advance, running, stacked)  56.1 us
    all_gather x1, waiting for transfers between devices, local(): piece_values = lax.all_gather(mark_values, 'tm', axis=0, tiled=True)  54.2 us
    all_to_all x1, waiting for transfers between devices, local(): lax.all_to_all(sent_rows, 'pack', split_axis=0, concat_axis=0, tiled=True)  45.8 us
  transfers between devices with their start and end apart: 4, of which 3 were waited for; matrix products, arithmetic and copies ran while one was open for 61% of the time, Pallas kernels for 0%

commit v1 on v0

v1 whole, which is shorter than its diff:
```python
import functools

import jax
import jax.numpy as jnp
from jax import lax
from jax.experimental import pallas as pl
from jax.experimental.pallas import tpu as pltpu
from jax.sharding import PartitionSpec as P

HEAD = 64
LANE = 128
LANDMARKS = 256
BLOCK = 128
WINDOW = 16
CAPACITY = 2
POOL_DEV = 128
F32 = jnp.float32
BF16 = jnp.bfloat16
I32 = jnp.int32
MESH = pl.DeviceIdType.MESH
EXP_SCALE = HEAD**-0.5 * 1.4426950408889634


def dot_t(a, b):
    return lax.dot_general(a, b, (((1,), (1,)), ((), ())), preferred_element_type=F32)


def dot(a, b):
    return jnp.dot(a, b, preferred_element_type=F32)


def swap_halves(x):
    return pltpu.roll(x, HEAD, 1)


def body(
    n_tm,
    n_pack,
    chunk,
    q_hbm,
    k_hbm,
    v_hbm,
    w_hbm,
    gain_ref,
    owner_ref,
    base_ref,
    offset_ref,
    enc_hbm,
    pooled_ref,
    q_v,
    k_v,
    v_v,
    w_v,
    mark_q,
    q_out,
    q_in,
    kv_out,
    kv_in,
    k_wide,
    v_wide,
    s_a,
    s_b,
    top_a,
    top_b,
    o_out,
    o_in,
    attended,
    enc_v,
    one_hot,
    tags_out,
    tags_in,
    pool_out,
    pool_in,
    load_sem,
    q_send,
    q_recv,
    kv_send,
    kv_recv,
    o_send,
    o_recv,
    tag_send,
    tag_recv,
    pool_send,
    pool_recv,
    store_sem,
):
    me = lax.axis_index("tm")
    pk = lax.axis_index("pack")
    frames, width = q_v.shape
    half_rows = frames // 2
    lands = n_tm * LANDMARKS
    pairs = width // LANE

    loads = [
        pltpu.make_async_copy(src.at[0] if i < 3 else src, dst, load_sem.at[i])
        for i, (src, dst) in enumerate(((q_hbm, q_v), (k_hbm, k_v), (v_hbm, v_v), (w_hbm, w_v)))
    ]
    for load in loads:
        load.start()

    barrier = pltpu.get_barrier_semaphore()

    def greet_tm(r, c):
        pl.semaphore_signal(
            barrier, inc=1, device_id={"tm": lax.rem(me + r, n_tm)}, device_id_type=MESH
        )
        return c

    def greet_pack(r, c):
        pl.semaphore_signal(
            barrier, inc=1, device_id={"pack": lax.rem(pk + r, n_pack)}, device_id_type=MESH
        )
        return c

    lax.fori_loop(1, n_tm, greet_tm, 0)
    lax.fori_loop(1, n_pack, greet_pack, 0)

    def tm_copy(src, dst, send, recv, peer, source):
        return pltpu.make_async_remote_copy(
            src_ref=src.at[peer],
            dst_ref=dst.at[source],
            send_sem=send.at[peer],
            recv_sem=recv.at[source],
            device_id={"tm": peer},
            device_id_type=MESH,
        )

    def pack_copy(src, dst, send, recv, peer, source):
        return pltpu.make_async_remote_copy(
            src_ref=src.at[peer],
            dst_ref=dst.at[source],
            send_sem=send.at[peer],
            recv_sem=recv.at[source],
            device_id={"pack": peer},
            device_id_type=MESH,
        )

    lane = lax.broadcasted_iota(I32, (half_rows, LANE), 1)
    low = lane < HEAD

    slot_rows = CAPACITY * WINDOW
    out_rows = n_pack * slot_rows
    n_blocks = offset_ref.shape[0]
    row_id = lax.broadcasted_iota(I32, (out_rows, LANE), 0)
    owner_id = row_id // slot_rows
    slot_id = (row_id // WINDOW) % CAPACITY
    window_id = row_id % WINDOW
    target = jnp.full((out_rows, LANE), -1, I32)
    tally = jnp.zeros((out_rows, LANE), F32)
    for b in range(n_blocks):
        owner = owner_ref[0, b]
        rank = jnp.int32(0)
        for earlier in range(b):
            rank = rank + jnp.where(owner_ref[0, earlier] == owner, 1, 0)
        mine = (owner_id == owner) & (slot_id == rank)
        target = jnp.where(mine, window_id + base_ref[0, b], target)
        hit = mine & (window_id == offset_ref[b : b + 1, :])
        hit = jnp.where(hit, 1.0, 0.0)
        tally = tally + jnp.sum(hit, axis=1, keepdims=True)
        one_hot[:, b * BLOCK : (b + 1) * BLOCK] = hit.astype(BF16)
    tag_lane = lax.broadcasted_iota(I32, (out_rows, LANE), 1)
    tags = jnp.where(tag_lane == 0, target.astype(F32), tally).astype(BF16)
    for o in range(n_pack):
        tags_out[o] = tags[o * slot_rows : (o + 1) * slot_rows, :]

    average = jnp.where(
        lax.broadcasted_iota(I32, (LANDMARKS, frames), 1) // 2
        == lax.broadcasted_iota(I32, (LANDMARKS, frames), 0),
        0.5,
        0.0,
    ).astype(BF16)

    loads[0].wait()

    def pack_queries(j, c):
        cols = pl.ds(pl.multiple_of(j * LANE, LANE), LANE)
        upper = q_v[0:half_rows, cols].astype(F32)
        lower = q_v[half_rows:frames, cols].astype(F32)
        q_out[2 * j] = jnp.where(low, upper, swap_halves(lower)).astype(BF16)
        q_out[2 * j + 1] = jnp.where(low, swap_halves(upper), lower).astype(BF16)
        mark_q[:, cols] = dot(average, q_v[:, cols]).astype(BF16)
        return c

    lax.fori_loop(0, pairs, pack_queries, 0)

    pl.semaphore_wait(barrier, n_tm + n_pack - 2)

    def send_queries(r, c):
        tm_copy(q_out, q_in, q_send, q_recv, lax.rem(me + r, n_tm), me).start()
        return c

    lax.fori_loop(1, n_tm, send_queries, 0)
    q_in[me] = q_out[me]

    def send_tags(r, c):
        pack_copy(tags_out, tags_in, tag_send, tag_recv, lax.rem(pk + r, n_pack), pk).start()
        return c

    lax.fori_loop(1, n_pack, send_tags, 0)
    tags_in[pk] = tags_out[pk]

    loads[1].wait()
    loads[2].wait()

    def summarize(step, c):
        j = lax.rem(me // 2 + step, pairs)
        cols = pl.ds(pl.multiple_of(j * LANE, LANE), LANE)
        keys = k_v[:, cols]
        mk = dot(average, keys).astype(BF16).astype(F32)
        mq = mark_q[:, cols].astype(F32)
        vals = v_v[:, cols]
        parts = []
        for head in range(2):
            chosen = low if head == 0 else ~low
            s = dot_t(jnp.where(chosen, mq, 0.0).astype(BF16), keys)
            p = jnp.exp2((s - jnp.max(s, axis=1, keepdims=True)) * EXP_SCALE)
            total = jnp.sum(p, axis=1, keepdims=True)
            parts.append(dot(p.astype(BF16), vals) / total)
        mv = jnp.where(low, parts[0], parts[1])
        kv_out[2 * j] = jnp.where(low, mk, swap_halves(mv)).astype(BF16)
        kv_out[2 * j + 1] = jnp.where(low, swap_halves(mk), mv).astype(BF16)
        for head in range(2):
            peer = 2 * j + head

            @pl.when(peer != me)
            def _():
                tm_copy(kv_out, kv_in, kv_send, kv_recv, peer, me).start()

            @pl.when(peer == me)
            def _():
                kv_in[me] = kv_out[me]

        return c

    lax.fori_loop(0, pairs, summarize, 0)

    def widen(i, c):
        source = lax.rem(me + n_tm - i, n_tm)

        @pl.when(source != me)
        def _():
            tm_copy(kv_out, kv_in, kv_send, kv_recv, source, source).wait_recv()

        rows = pl.ds(pl.multiple_of(source * LANDMARKS, LANDMARKS), LANDMARKS)
        straight = kv_in[source].astype(F32)
        swapped = swap_halves(straight)
        low_land = lax.broadcasted_iota(I32, (LANDMARKS, LANE), 1) < HEAD
        k_wide[0, rows, :] = jnp.where(low_land, straight, 0.0).astype(BF16)
        k_wide[1, rows, :] = jnp.where(low_land, 0.0, swapped).astype(BF16)
        v_wide[0, rows, :] = jnp.where(low_land, swapped, 1.0).astype(BF16)
        v_wide[1, rows, :] = jnp.where(low_land, 1.0, straight).astype(BF16)
        return c

    lax.fori_loop(0, n_tm, widen, 0)

    pieces = [slice(at, at + chunk) for at in range(0, lands, chunk)]

    def score_piece(q, half, piece, s_ref, top):
        s = dot_t(q, k_wide[half, piece, :])
        s_ref[:, piece] = s
        for at in range(0, chunk, LANE):
            part = s[:, at : at + LANE]
            top = part if top is None else jnp.maximum(top, part)
        return top

    def blend_piece(half, piece, s_ref, top, acc):
        p = jnp.exp2((s_ref[:, piece] - top) * EXP_SCALE).astype(BF16)
        d = dot(p, v_wide[half, piece, :])
        return d if acc is None else acc + d

    def stage(q, half_next, s_next, top_next, half, s_now, top_now):
        top = jnp.max(top_now[...], axis=1, keepdims=True)
        following, acc = None, None
        for piece in pieces:
            if q is not None:
                following = score_piece(q, half_next, piece, s_next, following)
            acc = blend_piece(half, piece, s_now, top, acc)
        if q is not None:
            top_next[...] = following
        return acc

    def finish(source, first, second):
        o = jnp.where(low, first / first[:, HEAD : HEAD + 1], second / second[:, 0:1])
        o_out[source] = o.astype(BF16)

    following = None
    for piece in pieces:
        following = score_piece(q_in[me], 0, piece, s_a, following)
    top_a[...] = following

    def attend(i, c):
        source = lax.rem(me + n_tm - i, n_tm)
        coming = lax.rem(me + n_tm - 1 - i, n_tm)
        tm_copy(q_out, q_in, q_send, q_recv, coming, coming).wait_recv()
        first = stage(q_in[source], 1, s_b, top_b, 0, s_a, top_a)
        second = stage(q_in[coming], 0, s_a, top_a, 1, s_b, top_b)
        finish(source, first, second)

        @pl.when(i > 0)
        def _():
            tm_copy(o_out, o_in, o_send, o_recv, source, me).start()

        return c

    lax.fori_loop(0, n_tm - 1, attend, 0)
    last = lax.rem(me + 1, n_tm)
    first = stage(q_in[last], 1, s_b, top_b, 0, s_a, top_a)
    second = stage(None, None, None, None, 1, s_b, top_b)
    finish(last, first, second)
    tm_copy(o_out, o_in, o_send, o_recv, last, me).start()
    o_in[me] = o_out[me]

    def await_heads(i, c):
        source = lax.rem(me + i, n_tm)
        tm_copy(o_out, o_in, o_send, o_recv, source, source).wait_recv()
        return c

    lax.fori_loop(1, n_tm, await_heads, 0)

    def unpack(j, c):
        cols = pl.ds(pl.multiple_of(j * LANE, LANE), LANE)
        even = o_in[2 * j].astype(F32)
        odd = o_in[2 * j + 1].astype(F32)
        attended[0:half_rows, cols] = jnp.where(low, even, swap_halves(odd)).astype(BF16)
        attended[half_rows:frames, cols] = jnp.where(low, swap_halves(even), odd).astype(BF16)
        return c

    lax.fori_loop(0, pairs, unpack, 0)
    loads[3].wait()
    gain = gain_ref[...]

    def project(i, c):
        rows = pl.ds(pl.multiple_of(i * BLOCK, BLOCK), BLOCK)
        projected = dot(attended[rows, :], w_v[...])
        power = jnp.mean(projected * projected, axis=1, keepdims=True)
        enc_v[rows, :] = (projected * lax.rsqrt(power + 1e-6) * gain).astype(BF16)
        return c

    lax.fori_loop(0, frames // BLOCK, project, 0)
    store = pltpu.make_async_copy(enc_v, enc_hbm.at[0], store_sem)
    store.start()

    summed = dot(one_hot[...], enc_v[...]).astype(BF16)
    for o in range(n_pack):
        pool_out[o] = summed[o * slot_rows : (o + 1) * slot_rows, :]

    def send_pool(r, c):
        pack_copy(pool_out, pool_in, pool_send, pool_recv, lax.rem(pk + r, n_pack), pk).start()
        return c

    lax.fori_loop(1, n_pack, send_pool, 0)
    pool_in[pk] = pool_out[pk]

    def await_pool(i, c):
        source = lax.rem(pk + i, n_pack)
        pack_copy(tags_out, tags_in, tag_send, tag_recv, source, source).wait_recv()
        pack_copy(pool_out, pool_in, pool_send, pool_recv, source, source).wait_recv()
        return c

    lax.fori_loop(1, n_pack, await_pool, 0)
    tags = tags_in[...].reshape(out_rows, LANE)
    rows = tags.astype(F32)[:, 0:1].astype(I32)
    placing = jnp.where(
        rows == lax.broadcasted_iota(I32, (out_rows, POOL_DEV), 1), 1.0, 0.0
    ).astype(BF16)
    contract = (((0,), (0,)), ((), ()))
    sums = lax.dot_general(
        placing, pool_in[...].reshape(out_rows, width), contract, preferred_element_type=F32
    )
    counts = lax.dot_general(placing, tags, contract, preferred_element_type=F32)[:, 1:2]
    pooled_ref[0] = (sums / jnp.maximum(counts, 1.0)).astype(BF16)

    def drain_tm(r, c):
        peer = lax.rem(me + r, n_tm)
        tm_copy(q_out, q_in, q_send, q_recv, peer, me).wait_send()
        tm_copy(kv_out, kv_in, kv_send, kv_recv, peer, me).wait_send()
        tm_copy(o_out, o_in, o_send, o_recv, peer, me).wait_send()
        return c

    def drain_pack(r, c):
        peer = lax.rem(pk + r, n_pack)
        pack_copy(tags_out, tags_in, tag_send, tag_recv, peer, pk).wait_send()
        pack_copy(pool_out, pool_in, pool_send, pool_recv, peer, pk).wait_send()
        return c

    lax.fori_loop(1, n_tm, drain_tm, 0)
    lax.fori_loop(1, n_pack, drain_pack, 0)
    store.wait()


def local(queries, keys, values, w_out, norm_gain, block_owner, block_base, frame_offset):
    n_tm = lax.axis_size("tm")
    n_pack = lax.axis_size("pack")
    _, frames, width = queries.shape
    lands = n_tm * LANDMARKS
    half = frames // 2
    slot_rows = CAPACITY * WINDOW
    any_ref = pl.BlockSpec(memory_space=pl.ANY)
    vmem = pl.BlockSpec(memory_space=pltpu.VMEM)
    smem = pl.BlockSpec(memory_space=pltpu.SMEM)
    dma = pltpu.SemaphoreType.DMA
    call = pl.pallas_call(
        functools.partial(body, n_tm, n_pack, min(1024, lands)),
        name="landmark_layer",
        out_shape=(
            jax.ShapeDtypeStruct((1, frames, width), BF16),
            jax.ShapeDtypeStruct((1, POOL_DEV, width), BF16),
        ),
        in_specs=[any_ref] * 4 + [vmem, smem, smem, vmem],
        out_specs=(any_ref, vmem),
        scratch_shapes=[
            pltpu.VMEM((frames, width), BF16),
            pltpu.VMEM((frames, width), BF16),
            pltpu.VMEM((frames, width), BF16),
            pltpu.VMEM((width, width), BF16),
            pltpu.VMEM((LANDMARKS, width), BF16),
            pltpu.VMEM((n_tm, half, LANE), BF16),
            pltpu.VMEM((n_tm, half, LANE), BF16),
            pltpu.VMEM((n_tm, LANDMARKS, LANE), BF16),
            pltpu.VMEM((n_tm, LANDMARKS, LANE), BF16),
            pltpu.VMEM((2, lands, LANE), BF16),
            pltpu.VMEM((2, lands, LANE), BF16),
            pltpu.VMEM((half, lands), F32),
            pltpu.VMEM((half, lands), F32),
            pltpu.VMEM((half, LANE), F32),
            pltpu.VMEM((half, LANE), F32),
            pltpu.VMEM((n_tm, half, LANE), BF16),
            pltpu.VMEM((n_tm, half, LANE), BF16),
            pltpu.VMEM((frames, width), BF16),
            pltpu.VMEM((frames, width), BF16),
            pltpu.VMEM((n_pack * slot_rows, frames), BF16),
            pltpu.VMEM((n_pack, slot_rows, LANE), BF16),
            pltpu.VMEM((n_pack, slot_rows, LANE), BF16),
            pltpu.VMEM((n_pack, slot_rows, width), BF16),
            pltpu.VMEM((n_pack, slot_rows, width), BF16),
            dma((4,)),
            dma((n_tm,)),
            dma((n_tm,)),
            dma((n_tm,)),
            dma((n_tm,)),
            dma((n_tm,)),
            dma((n_tm,)),
            dma((n_pack,)),
            dma((n_pack,)),
            dma((n_pack,)),
            dma((n_pack,)),
            dma(()),
        ],
        compiler_params=pltpu.CompilerParams(
            collective_id=0, has_side_effects=True, vmem_limit_bytes=56 << 20
        ),
        cost_estimate=pl.CostEstimate(
            flops=20_000_000_000, bytes_accessed=8_000_000, transcendentals=36_000_000
        ),
    )
    return call(
        queries,
        keys,
        values,
        w_out,
        norm_gain.reshape(1, width),
        block_owner.reshape(1, -1),
        block_base,
        frame_offset[0],
    )


def solution(mesh):
    return jax.shard_map(
        local,
        mesh=mesh,
        in_specs=(
            P("pack", "tm", None),
            P("pack", "tm", None),
            P("pack", "tm", None),
            P(),
            P(),
            P("pack", "tm", None),
            P("pack", "tm"),
            P("pack", "tm", None),
        ),
        out_specs=(P("pack", "tm", None), P("pack", "tm", None)),
        check_vma=False,
    )
```

time: 599 us -> 100 us (0.17)
  matrix products: 215 us -> 0 us
  waiting for transfers between devices: 173 us -> 0 us
  other arithmetic: 105 us -> 0 us
  Pallas kernels: 0 us -> 96.2 us
  local copies, waits for them, and re-layouts: 77.1 us -> 3.01 us
  between operations: 14.2 us -> 0.65 us
  starting transfers between devices: 11.1 us -> 0 us
    dot_general x36 -> x0, matrix products: 215 us -> none  [the longest x16 113 us: absorb(): jnp.einsum('nhm,mhe->nhe', weights.astype(jnp.bfloat16), value_heads, pre...]
    all_gather x2 -> x0, waiting for transfers between devices: 127 us -> none  [the longest x1 72.6 us: local(): piece_keys = lax.all_gather(mark_keys, 'tm', axis=0, tiled=True)]
    pallas_call x0 -> x1, Pallas kernels: none -> 96.2 us  [local(): call(queries, keys, values, w_out, norm_gain.reshape(1, width), block_own...]
    reduce_sum x22 -> x0, other arithmetic: 89.7 us -> none  [the longest x16 77.1 us: absorb(): running_sum = running_sum * rescale + jnp.sum(weights, axis=-1)]
    dynamic_slice x48 -> x0, local copies, waits for them, and re-layouts: 56.1 us -> none  [local(): running, unused = lax.scan(advance, running, stacked)]
    all_to_all x2 -> x0, waiting for transfers between devices: 45.9 us -> none  [the longest x1 45.8 us: local(): lax.all_to_all(sent_rows, 'pack', split_axis=0, concat_axis=0, tiled=True)]
    all_to_all x2 -> x0, starting transfers between devices: 11.1 us -> none  [the longest x1 5.97 us: local(): lax.all_to_all(sent_targets, 'pack', split_axis=0, concat_axis=0, tiled=T...]
    convert_element_type x4 -> x0, local copies, waits for them, and re-layouts: 9.99 us -> none  [the longest x1 3.58 us: local(): jnp.mean(frame_q.reshape(LANDMARKS, span, model_width), axis=1, dtype=jnp...]
  transfers between devices with their start and end apart: 4 -> 0, of which waited for: 3 -> 0; matrix products, arithmetic and copies ran while one was open for 61% -> 0% of each run, Pallas kernels for 0% -> 0%
where the time goes in v1:
time: 100 us; the launch traced here: 99.9 us
  Pallas kernels  96.2 us (96%)
  local copies, waits for them, and re-layouts  3.01 us (3%)
    pallas_call x1, Pallas kernels, local(): call(queries, keys, values, w_out, norm_gain.reshape(1, width), block_own...  96.2 us
    unnamed x4, local copies, waits for them, and re-layouts  3.01 us

profile of v1, /device:TPU:1, one launch (start us, length us, event | category | flops | bytes accessed | tf_op | source)
XLA Modules:
  0.0 99.9 jit_solution(15466317494548411528)
XLA Ops:
  0.6 96.2 %landmark_layer.1 = (bf16[1,512,1024]{2,1,0:T(8,128)(2,1)}, bf16[1,128,1024]{2,1,0:T(8,128)(2,1)}) custom-call(bf16[1,512,1024]{2,1,0:T(8,128)(2,1)} %q_hbm.1, bf16[1,512,1024]{2,1,0:T(8,128)(2,1)} %k_hbm.1, bf16[1,512,1024]{2,1,0:T(8,128)(2,1)} %v_hbm.1, bf16[1024,1024]{1,0:T(8,128)(2,1)} %w_hbm.1, f32[1,1024]{1,0:T(1,128)} %bitcast.3, s32[1,4]{1,0:T(1,128)} %bitcast.5, ...), custom_call_target="tpu_custom_call" | custom-call | flops 20000000000 | bytes 8000000 | tf_op jit(solution)/shard_map/landmark_layer/pallas_call | solution.py:456
  96.8 0.0 copy-start
  96.8 2.3 %copy.12 = bf16[1,512,1024]{2,1,0:T(8,128)(2,1)} copy(bf16[1,512,1024]{2,1,0:T(8,128)(2,1)} %get-tuple-element.4) | data formatting | bytes 2097152
  99.1 0.0 copy-done
  99.2 0.7 copy.13
Async XLA Ops:
  96.8 2.3 %copy-start = (bf16[1,128,1024]{2,1,0:T(8,128)(2,1)S(1)}, bf16[1,128,1024]{2,1,0:T(8,128)(2,1)}, u32[]{:S(2)}) copy-start(bf16[1,128,1024]{2,1,0:T(8,128)(2,1)} %get-tuple-element.5) | copy-start | bytes 786436

commit v2 on v1

--- a/solution.py
+++ b/solution.py
@@ -51,11 +51,12 @@
     k_v,
     v_v,
     w_v,
-    mark_q,
     q_out,
     q_in,
-    kv_out,
-    kv_in,
+    k_out,
+    k_in,
+    v_out,
+    v_in,
     k_wide,
     v_wide,
     s_a,
@@ -74,8 +75,10 @@
     load_sem,
     q_send,
     q_recv,
-    kv_send,
-    kv_recv,
+    k_send,
+    k_recv,
+    v_send,
+    v_recv,
     o_send,
     o_recv,
     tag_send,
@@ -93,7 +96,7 @@
 
     loads = [
         pltpu.make_async_copy(src.at[0] if i < 3 else src, dst, load_sem.at[i])
-        for i, (src, dst) in enumerate(((q_hbm, q_v), (k_hbm, k_v), (v_hbm, v_v), (w_hbm, w_v)))
+        for i, (src, dst) in enumerate(((k_hbm, k_v), (q_hbm, q_v), (v_hbm, v_v), (w_hbm, w_v)))
     ]
     for load in loads:
         load.start()
@@ -170,45 +173,49 @@
         0.0,
     ).astype(BF16)
 
+    land_rows = LANDMARKS // 2
+    low_land = lax.broadcasted_iota(I32, (land_rows, LANE), 1) < HEAD
+
+    def fold(ref, j, x, mask):
+        upper, lower = x[: x.shape[0] // 2], x[x.shape[0] // 2 :]
+        ref[2 * j] = jnp.where(mask, upper, swap_halves(lower)).astype(BF16)
+        ref[2 * j + 1] = jnp.where(mask, swap_halves(upper), lower).astype(BF16)
+
+    def pair_columns(j):
+        return pl.ds(pl.multiple_of(j * LANE, LANE), LANE)
+
     loads[0].wait()
 
+    def mark_keys(j, c):
+        means = dot(average, k_v[:, pair_columns(j)])
+        fold(k_out, j, means.astype(BF16).astype(F32), low_land)
+        return c
+
+    lax.fori_loop(0, pairs, mark_keys, 0)
+    loads[1].wait()
+
     def pack_queries(j, c):
-        cols = pl.ds(pl.multiple_of(j * LANE, LANE), LANE)
-        upper = q_v[0:half_rows, cols].astype(F32)
-        lower = q_v[half_rows:frames, cols].astype(F32)
-        q_out[2 * j] = jnp.where(low, upper, swap_halves(lower)).astype(BF16)
-        q_out[2 * j + 1] = jnp.where(low, swap_halves(upper), lower).astype(BF16)
-        mark_q[:, cols] = dot(average, q_v[:, cols]).astype(BF16)
+        fold(q_out, j, q_v[:, pair_columns(j)].astype(F32), low)
         return c
 
     lax.fori_loop(0, pairs, pack_queries, 0)
 
     pl.semaphore_wait(barrier, n_tm + n_pack - 2)
 
-    def send_queries(r, c):
-        tm_copy(q_out, q_in, q_send, q_recv, lax.rem(me + r, n_tm), me).start()
-        return c
-
-    lax.fori_loop(1, n_tm, send_queries, 0)
-    q_in[me] = q_out[me]
-
-    def send_tags(r, c):
-        pack_copy(tags_out, tags_in, tag_send, tag_recv, lax.rem(pk + r, n_pack), pk).start()
-        return c
-
-    lax.fori_loop(1, n_pack, send_tags, 0)
-    tags_in[pk] = tags_out[pk]
-
-    loads[1].wait()
+    def send_keys(r, c):
+        tm_copy(k_out, k_in, k_send, k_recv, lax.rem(me + r, n_tm), me).start()
+        return c
+
+    lax.fori_loop(1, n_tm, send_keys, 0)
+    k_in[me] = k_out[me]
+
     loads[2].wait()
 
     def summarize(step, c):
         j = lax.rem(me // 2 + step, pairs)
-        cols = pl.ds(pl.multiple_of(j * LANE, LANE), LANE)
-        keys = k_v[:, cols]
-        mk = dot(average, keys).astype(BF16).astype(F32)
-        mq = mark_q[:, cols].astype(F32)
-        vals = v_v[:, cols]
+        cols = pair_columns(j)
+        keys, vals = k_v[:, cols], v_v[:, cols]
+        mq = dot(average, q_v[:, cols])
         parts = []
         for head in range(2):
             chosen = low if head == 0 else ~low
@@ -216,42 +223,55 @@
             p = jnp.exp2((s - jnp.max(s, axis=1, keepdims=True)) * EXP_SCALE)
             total = jnp.sum(p, axis=1, keepdims=True)
             parts.append(dot(p.astype(BF16), vals) / total)
-        mv = jnp.where(low, parts[0], parts[1])
-        kv_out[2 * j] = jnp.where(low, mk, swap_halves(mv)).astype(BF16)
-        kv_out[2 * j + 1] = jnp.where(low, swap_halves(mk), mv).astype(BF16)
+        fold(v_out, j, jnp.where(low, parts[0], parts[1]), low_land)
         for head in range(2):
             peer = 2 * j + head
 
             @pl.when(peer != me)
             def _():
-                tm_copy(kv_out, kv_in, kv_send, kv_recv, peer, me).start()
-
-            @pl.when(peer == me)
+                tm_copy(v_out, v_in, v_send, v_recv, peer, me).start()
+
+        return c
+
+    lax.fori_loop(0, pairs, summarize, 0)
+    v_in[me] = v_out[me]
+
+    def send_queries(r, c):
+        tm_copy(q_out, q_in, q_send, q_recv, lax.rem(me + r, n_tm), me).start()
+        return c
+
+    lax.fori_loop(1, n_tm, send_queries, 0)
+    q_in[me] = q_out[me]
+
+    def send_tags(r, c):
+        pack_copy(tags_out, tags_in, tag_send, tag_recv, lax.rem(pk + r, n_pack), pk).start()
+        return c
+
+    lax.fori_loop(1, n_pack, send_tags, 0)
+    tags_in[pk] = tags_out[pk]
+
+    def widen(arrived, send, recv, out, wide, filler):
+        def one(i, c):
+            source = lax.rem(me + n_tm - i, n_tm)
+
+            @pl.when(source != me)
             def _():
-                kv_in[me] = kv_out[me]
-
-        return c
-
-    lax.fori_loop(0, pairs, summarize, 0)
-
-    def widen(i, c):
-        source = lax.rem(me + n_tm - i, n_tm)
-
-        @pl.when(source != me)
-        def _():
-            tm_copy(kv_out, kv_in, kv_send, kv_recv, source, source).wait_recv()
-
-        rows = pl.ds(pl.multiple_of(source * LANDMARKS, LANDMARKS), LANDMARKS)
-        straight = kv_in[source].astype(F32)
-        swapped = swap_halves(straight)
-        low_land = lax.broadcasted_iota(I32, (LANDMARKS, LANE), 1) < HEAD
-        k_wide[0, rows, :] = jnp.where(low_land, straight, 0.0).astype(BF16)
-        k_wide[1, rows, :] = jnp.where(low_land, 0.0, swapped).astype(BF16)
-        v_wide[0, rows, :] = jnp.where(low_land, swapped, 1.0).astype(BF16)
-        v_wide[1, rows, :] = jnp.where(low_land, 1.0, straight).astype(BF16)
-        return c
-
-    lax.fori_loop(0, n_tm, widen, 0)
+                tm_copy(out, arrived, send, recv, source, source).wait_recv()
+
+            at = pl.multiple_of(source * LANDMARKS, LANDMARKS)
+            upper = pl.ds(at, land_rows)
+            lower = pl.ds(at + land_rows, land_rows)
+            straight = arrived[source].astype(F32)
+            swapped = swap_halves(straight)
+            wide[0, upper, :] = jnp.where(low_land, straight, filler).astype(BF16)
+            wide[0, lower, :] = jnp.where(low_land, swapped, filler).astype(BF16)
+            wide[1, upper, :] = jnp.where(low_land, filler, swapped).astype(BF16)
+            wide[1, lower, :] = jnp.where(low_land, filler, straight).astype(BF16)
+            return c
+
+        lax.fori_loop(0, n_tm, one, 0)
+
+    widen(k_in, k_send, k_recv, k_out, k_wide, 0.0)
 
     pieces = [slice(at, at + chunk) for at in range(0, lands, chunk)]
 
@@ -287,6 +307,7 @@
     for piece in pieces:
         following = score_piece(q_in[me], 0, piece, s_a, following)
     top_a[...] = following
+    widen(v_in, v_send, v_recv, v_out, v_wide, 1.0)
 
     def attend(i, c):
         source = lax.rem(me + n_tm - i, n_tm)
@@ -330,13 +351,13 @@
     gain = gain_ref[...]
 
     def project(i, c):
-        rows = pl.ds(pl.multiple_of(i * BLOCK, BLOCK), BLOCK)
+        rows = pl.ds(pl.multiple_of(i * half_rows, half_rows), half_rows)
         projected = dot(attended[rows, :], w_v[...])
         power = jnp.mean(projected * projected, axis=1, keepdims=True)
         enc_v[rows, :] = (projected * lax.rsqrt(power + 1e-6) * gain).astype(BF16)
         return c
 
-    lax.fori_loop(0, frames // BLOCK, project, 0)
+    lax.fori_loop(0, 2, project, 0)
     store = pltpu.make_async_copy(enc_v, enc_hbm.at[0], store_sem)
     store.start()
 
@@ -373,7 +394,8 @@
     def drain_tm(r, c):
         peer = lax.rem(me + r, n_tm)
         tm_copy(q_out, q_in, q_send, q_recv, peer, me).wait_send()
-        tm_copy(kv_out, kv_in, kv_send, kv_recv, peer, me).wait_send()
+        tm_copy(k_out, k_in, k_send, k_recv, peer, me).wait_send()
+        tm_copy(v_out, v_in, v_send, v_recv, peer, me).wait_send()
         tm_copy(o_out, o_in, o_send, o_recv, peer, me).wait_send()
         return c
 
@@ -413,11 +435,12 @@
             pltpu.VMEM((frames, width), BF16),
             pltpu.VMEM((frames, width), BF16),
             pltpu.VMEM((width, width), BF16),
-            pltpu.VMEM((LANDMARKS, width), BF16),
             pltpu.VMEM((n_tm, half, LANE), BF16),
             pltpu.VMEM((n_tm, half, LANE), BF16),
-            pltpu.VMEM((n_tm, LANDMARKS, LANE), BF16),
-            pltpu.VMEM((n_tm, LANDMARKS, LANE), BF16),
+            pltpu.VMEM((n_tm, LANDMARKS // 2, LANE), BF16),
+            pltpu.VMEM((n_tm, LANDMARKS // 2, LANE), BF16),
+            pltpu.VMEM((n_tm, LANDMARKS // 2, LANE), BF16),
+            pltpu.VMEM((n_tm, LANDMARKS // 2, LANE), BF16),
             pltpu.VMEM((2, lands, LANE), BF16),
             pltpu.VMEM((2, lands, LANE), BF16),
             pltpu.VMEM((half, lands), F32),
@@ -434,6 +457,8 @@
             pltpu.VMEM((n_pack, slot_rows, width), BF16),
             pltpu.VMEM((n_pack, slot_rows, width), BF16),
             dma((4,)),
+            dma((n_tm,)),
+            dma((n_tm,)),
             dma((n_tm,)),
             dma((n_tm,)),
             dma((n_tm,)),

time: 100 us -> 89.3 us (0.89)
  the two profiles are of different devices: /device:TPU:1 before, /device:TPU:67 now
where the time goes in v2:
time: 89.3 us; the launch traced here: 89.2 us
  Pallas kernels  85.5 us (96%)
  local copies, waits for them, and re-layouts  3.01 us (3%)
    pallas_call x1, Pallas kernels, local(): call(queries, keys, values, w_out, norm_gain.reshape(1, width), block_own...  85.5 us
    unnamed x4, local copies, waits for them, and re-layouts  3.01 us

profile of v2, /device:TPU:67, one launch (start us, length us, event | category | flops | bytes accessed | tf_op | source)
XLA Modules:
  0.0 89.2 jit_solution(5535415591929632596)
XLA Ops:
  0.6 85.5 %landmark_layer.1 = (bf16[1,512,1024]{2,1,0:T(8,128)(2,1)}, bf16[1,128,1024]{2,1,0:T(8,128)(2,1)}) custom-call(bf16[1,512,1024]{2,1,0:T(8,128)(2,1)} %q_hbm.1, bf16[1,512,1024]{2,1,0:T(8,128)(2,1)} %k_hbm.1, bf16[1,512,1024]{2,1,0:T(8,128)(2,1)} %v_hbm.1, bf16[1024,1024]{1,0:T(8,128)(2,1)} %w_hbm.1, f32[1,1024]{1,0:T(1,128)} %bitcast.3, s32[1,4]{1,0:T(1,128)} %bitcast.5, ...), custom_call_target="tpu_custom_call" | custom-call | flops 20000000000 | bytes 8000000 | tf_op jit(solution)/shard_map/landmark_layer/pallas_call | solution.py:481
  86.2 0.0 copy-start
  86.2 2.3 %copy.12 = bf16[1,512,1024]{2,1,0:T(8,128)(2,1)} copy(bf16[1,512,1024]{2,1,0:T(8,128)(2,1)} %get-tuple-element.4) | data formatting | bytes 2097152
  88.5 0.0 copy-done
  88.5 0.7 copy.13
Async XLA Ops:
  86.2 2.3 %copy-start = (bf16[1,128,1024]{2,1,0:T(8,128)(2,1)S(1)}, bf16[1,128,1024]{2,1,0:T(8,128)(2,1)}, u32[]{:S(2)}) copy-start(bf16[1,128,1024]{2,1,0:T(8,128)(2,1)} %get-tuple-element.5) | copy-start | bytes 786436

commit v3 on v2

v3 whole, which is shorter than its diff:
```python
import functools

import jax
import jax.numpy as jnp
from jax import lax
from jax.experimental import pallas as pl
from jax.experimental.pallas import tpu as pltpu
from jax.sharding import PartitionSpec as P

HEAD = 64
LANE = 128
LANDMARKS = 256
BLOCK = 128
WINDOW = 16
CAPACITY = 2
POOL_DEV = 128
F32 = jnp.float32
BF16 = jnp.bfloat16
I32 = jnp.int32
MESH = pl.DeviceIdType.MESH
EXP_SCALE = HEAD**-0.5 * 1.4426950408889634


def dot_t(a, b):
    return lax.dot_general(a, b, (((1,), (1,)), ((), ())), preferred_element_type=F32)


def dot(a, b):
    return jnp.dot(a, b, preferred_element_type=F32)


def swap_halves(x):
    return pltpu.roll(x, HEAD, 1)


def body(
    n_tm,
    n_pack,
    chunk,
    q_hbm,
    k_hbm,
    v_hbm,
    w_hbm,
    gain_ref,
    owner_ref,
    base_ref,
    offset_ref,
    enc_hbm,
    pooled_ref,
    q_v,
    k_v,
    v_v,
    w_v,
    q_out,
    q_in,
    k_out,
    k_in,
    v_out,
    v_in,
    k_wide,
    v_wide,
    s_a,
    s_b,
    top_a,
    top_b,
    o_out,
    o_in,
    attended,
    enc_v,
    one_hot,
    tags_out,
    tags_in,
    pool_out,
    pool_in,
    load_sem,
    q_send,
    q_recv,
    k_send,
    k_recv,
    v_send,
    v_recv,
    o_send,
    o_recv,
    tag_send,
    tag_recv,
    pool_send,
    pool_recv,
    store_sem,
):
    me = lax.axis_index("tm")
    pk = lax.axis_index("pack")
    frames, width = q_v.shape
    half_rows = frames // 2
    land_rows = LANDMARKS // 2
    pairs = n_tm // 2
    lands = n_tm * LANDMARKS

    loads = [
        pltpu.make_async_copy(src.at[0] if i < 3 else src, dst, load_sem.at[i])
        for i, (src, dst) in enumerate(((k_hbm, k_v), (q_hbm, q_v), (v_hbm, v_v), (w_hbm, w_v)))
    ]
    for load in loads:
        load.start()

    barrier = pltpu.get_barrier_semaphore()

    def greet_tm(r, c):
        pl.semaphore_signal(
            barrier, inc=1, device_id={"tm": lax.rem(me + r, n_tm)}, device_id_type=MESH
        )
        return c

    def greet_pack(r, c):
        pl.semaphore_signal(
            barrier, inc=1, device_id={"pack": lax.rem(pk + r, n_pack)}, device_id_type=MESH
        )
        return c

    lax.fori_loop(1, n_tm, greet_tm, 0)
    lax.fori_loop(1, n_pack, greet_pack, 0)

    def tm_copy(buffers, peer, source):
        src, dst, send, recv = buffers
        return pltpu.make_async_remote_copy(
            src_ref=src.at[peer],
            dst_ref=dst.at[source],
            send_sem=send.at[peer],
            recv_sem=recv.at[source],
            device_id={"tm": peer},
            device_id_type=MESH,
        )

    def pack_copy(buffers, peer, source):
        src, dst, send, recv = buffers
        return pltpu.make_async_remote_copy(
            src_ref=src.at[peer],
            dst_ref=dst.at[source],
            send_sem=send.at[peer],
            recv_sem=recv.at[source],
            device_id={"pack": peer},
            device_id_type=MESH,
        )

    queries = (q_out, q_in, q_send, q_recv)
    keys = (k_out, k_in, k_send, k_recv)
    values = (v_out, v_in, v_send, v_recv)
    results = (o_out, o_in, o_send, o_recv)
    tags = (tags_out, tags_in, tag_send, tag_recv)
    pools = (pool_out, pool_in, pool_send, pool_recv)

    def target_pair(t):
        return lax.rem(me // 2 + t, pairs)

    def source_pair(t):
        return lax.rem(me // 2 + pairs - t, pairs)

    def send_pair(buffers, pair):
        for member in range(2):
            peer = 2 * pair + member

            @pl.when(peer != me)
            def _():
                tm_copy(buffers, peer, me).start()

    def await_pair(buffers, pair):
        for member in range(2):
            source = 2 * pair + member

            @pl.when(source != me)
            def _():
                tm_copy(buffers, source, source).wait_recv()

    def send_steps(buffers, first, last):
        def one(t, c):
            send_pair(buffers, target_pair(t))
            return c

        lax.fori_loop(first, last, one, 0)

    low = lax.broadcasted_iota(I32, (half_rows, LANE), 1) < HEAD
    low_land = lax.broadcasted_iota(I32, (land_rows, LANE), 1) < HEAD

    def fold(ref, pair, x, mask):
        upper, lower = x[: x.shape[0] // 2], x[x.shape[0] // 2 :]
        ref[2 * pair] = jnp.where(mask, upper, swap_halves(lower)).astype(BF16)
        ref[2 * pair + 1] = jnp.where(mask, swap_halves(upper), lower).astype(BF16)

    def pair_columns(pair):
        return pl.ds(pl.multiple_of(pair * LANE, LANE), LANE)

    average = jnp.where(
        lax.broadcasted_iota(I32, (LANDMARKS, frames), 1) // 2
        == lax.broadcasted_iota(I32, (LANDMARKS, frames), 0),
        0.5,
        0.0,
    ).astype(BF16)

    loads[0].wait()
    per_dot = 2 if pairs % 2 == 0 else 1
    for first in range(0, pairs, per_dot):
        means = dot(average, k_v[:, first * LANE : (first + per_dot) * LANE])
        means = means.astype(BF16).astype(F32)
        for at in range(per_dot):
            fold(k_out, first + at, means[:, at * LANE : (at + 1) * LANE], low_land)
    k_in[me] = k_out[me]
    pl.semaphore_wait(barrier, n_tm + n_pack - 2)
    send_steps(keys, 0, pairs)

    loads[1].wait()
    loads[2].wait()

    def summarize(t):
        pair = target_pair(t)
        cols = pair_columns(pair)
        q, k, v = q_v[:, cols], k_v[:, cols], v_v[:, cols]
        mq = dot(average, q)
        parts = []
        for head in range(2):
            chosen = low if head == 0 else ~low
            s = dot_t(jnp.where(chosen, mq, 0.0).astype(BF16), k)
            p = jnp.exp2((s - jnp.max(s, axis=1, keepdims=True)) * EXP_SCALE)
            total = jnp.sum(p, axis=1, keepdims=True)
            parts.append(dot(p.astype(BF16), v) / total)
        fold(v_out, pair, jnp.where(low, parts[0], parts[1]), low_land)
        fold(q_out, pair, q.astype(F32), low)

    def send_values(t, c):
        summarize(t)
        send_pair(values, target_pair(t))
        return c

    lax.fori_loop(0, pairs, send_values, 0)
    v_in[me] = v_out[me]
    q_in[me] = q_out[me]
    send_steps(queries, 0, pairs)

    slot_rows = CAPACITY * WINDOW
    out_rows = n_pack * slot_rows
    n_blocks = offset_ref.shape[0]
    row_id = lax.broadcasted_iota(I32, (out_rows, LANE), 0)
    owner_id = row_id // slot_rows
    slot_id = (row_id // WINDOW) % CAPACITY
    window_id = row_id % WINDOW
    target = jnp.full((out_rows, LANE), -1, I32)
    tally = jnp.zeros((out_rows, LANE), F32)
    for b in range(n_blocks):
        owner = owner_ref[0, b]
        rank = jnp.int32(0)
        for earlier in range(b):
            rank = rank + jnp.where(owner_ref[0, earlier] == owner, 1, 0)
        mine = (owner_id == owner) & (slot_id == rank)
        target = jnp.where(mine, window_id + base_ref[0, b], target)
        hit = mine & (window_id == offset_ref[b : b + 1, :])
        hit = jnp.where(hit, 1.0, 0.0)
        tally = tally + jnp.sum(hit, axis=1, keepdims=True)
        one_hot[:, b * BLOCK : (b + 1) * BLOCK] = hit.astype(BF16)
    tag_lane = lax.broadcasted_iota(I32, (out_rows, LANE), 1)
    tag = jnp.where(tag_lane == 0, target.astype(F32), tally).astype(BF16)
    for o in range(n_pack):
        tags_out[o] = tag[o * slot_rows : (o + 1) * slot_rows, :]
    tags_in[pk] = tags_out[pk]

    def send_tags(r, c):
        pack_copy(tags, lax.rem(pk + r, n_pack), pk).start()
        return c

    lax.fori_loop(1, n_pack, send_tags, 0)

    def widen(buffers, t, wide, filler):
        pair = source_pair(t)
        await_pair(buffers, pair)
        for member in range(2):
            at = pl.multiple_of((2 * t + member) * LANDMARKS, LANDMARKS)
            upper = pl.ds(at, land_rows)
            lower = pl.ds(at + land_rows, land_rows)
            straight = buffers[1][2 * pair + member].astype(F32)
            swapped = swap_halves(straight)
            wide[0, upper, :] = jnp.where(low_land, straight, filler).astype(BF16)
            wide[0, lower, :] = jnp.where(low_land, swapped, filler).astype(BF16)
            wide[1, upper, :] = jnp.where(low_land, filler, swapped).astype(BF16)
            wide[1, lower, :] = jnp.where(low_land, filler, straight).astype(BF16)

    def widen_keys(t, c):
        widen(keys, t, k_wide, 0.0)
        return c

    def widen_values(t, c):
        widen(values, t, v_wide, 1.0)
        return c

    lax.fori_loop(0, pairs, widen_keys, 0)

    pieces = [slice(at, at + chunk) for at in range(0, lands, chunk)]

    def frames_of(t):
        both = q_in[pl.ds(pl.multiple_of(2 * source_pair(t), 2), 2)]
        return both.reshape(2 * half_rows, LANE)

    def score_piece(q, half, piece, s_ref, top):
        s = dot_t(q, k_wide[half, piece, :])
        s_ref[:, piece] = s
        for at in range(0, chunk, LANE):
            part = s[:, at : at + LANE]
            top = part if top is None else jnp.maximum(top, part)
        return top

    def blend_piece(half, piece, s_ref, top, acc):
        p = jnp.exp2((s_ref[:, piece] - top) * EXP_SCALE).astype(BF16)
        d = dot(p, v_wide[half, piece, :])
        return d if acc is None else acc + d

    def stage(q, half_next, s_next, top_next, half, s_now, top_now):
        top = jnp.max(top_now[...], axis=1, keepdims=True)
        following, acc = None, None
        for piece in pieces:
            if q is not None:
                following = score_piece(q, half_next, piece, s_next, following)
            acc = blend_piece(half, piece, s_now, top, acc)
        if q is not None:
            top_next[...] = following
        return acc

    low_both = lax.broadcasted_iota(I32, (2 * half_rows, LANE), 1) < HEAD

    def finish(t, first, second):
        o = jnp.where(low_both, first / first[:, HEAD : HEAD + 1], second / second[:, 0:1])
        o = o.astype(BF16)
        pair = source_pair(t)
        for member in range(2):
            o_out[2 * pair + member] = o[member * half_rows : (member + 1) * half_rows]
        send_pair(results, pair)

    await_pair(queries, source_pair(0))
    q_start = frames_of(0)
    following = None
    for piece in pieces:
        following = score_piece(q_start, 0, piece, s_a, following)
    top_a[...] = following
    lax.fori_loop(0, pairs, widen_values, 0)

    def attend(t, c):
        await_pair(queries, source_pair(t + 1))
        first = stage(frames_of(t), 1, s_b, top_b, 0, s_a, top_a)
        second = stage(frames_of(t + 1), 0, s_a, top_a, 1, s_b, top_b)
        finish(t, first, second)
        return c

    lax.fori_loop(0, pairs - 1, attend, 0)
    first = stage(frames_of(pairs - 1), 1, s_b, top_b, 0, s_a, top_a)
    second = stage(None, None, None, None, 1, s_b, top_b)
    finish(pairs - 1, first, second)
    o_in[me] = o_out[me]

    def unpack(t, c):
        pair = source_pair(t)
        await_pair(results, pair)
        cols = pair_columns(pair)
        even = o_in[2 * pair].astype(F32)
        odd = o_in[2 * pair + 1].astype(F32)
        attended[0:half_rows, cols] = jnp.where(low, even, swap_halves(odd)).astype(BF16)
        attended[half_rows:frames, cols] = jnp.where(low, swap_halves(even), odd).astype(BF16)
        return c

    lax.fori_loop(0, pairs, unpack, 0)
    loads[3].wait()
    gain = gain_ref[...]

    def project(i, c):
        rows = pl.ds(pl.multiple_of(i * half_rows, half_rows), half_rows)
        projected = dot(attended[rows, :], w_v[...])
        power = jnp.mean(projected * projected, axis=1, keepdims=True)
        enc_v[rows, :] = (projected * lax.rsqrt(power + 1e-6) * gain).astype(BF16)
        return c

    lax.fori_loop(0, 2, project, 0)
    store = pltpu.make_async_copy(enc_v, enc_hbm.at[0], store_sem)
    store.start()

    summed = dot(one_hot[...], enc_v[...]).astype(BF16)
    for o in range(n_pack):
        pool_out[o] = summed[o * slot_rows : (o + 1) * slot_rows, :]
    pool_in[pk] = pool_out[pk]

    def send_pool(r, c):
        pack_copy(pools, lax.rem(pk + r, n_pack), pk).start()
        return c

    lax.fori_loop(1, n_pack, send_pool, 0)

    def drain_tm(r, c):
        peer = lax.rem(me + r, n_tm)
        for buffers in (queries, keys, values, results):
            tm_copy(buffers, peer, me).wait_send()
        return c

    lax.fori_loop(1, n_tm, drain_tm, 0)

    def await_pool(i, c):
        source = lax.rem(pk + i, n_pack)
        pack_copy(tags, source, source).wait_recv()
        pack_copy(pools, source, source).wait_recv()
        return c

    lax.fori_loop(1, n_pack, await_pool, 0)
    tag = tags_in[...].reshape(out_rows, LANE)
    rows = tag.astype(F32)[:, 0:1].astype(I32)
    placing = jnp.where(
        rows == lax.broadcasted_iota(I32, (out_rows, POOL_DEV), 1), 1.0, 0.0
    ).astype(BF16)
    contract = (((0,), (0,)), ((), ()))
    sums = lax.dot_general(
        placing, pool_in[...].reshape(out_rows, width), contract, preferred_element_type=F32
    )
    counts = lax.dot_general(placing, tag, contract, preferred_element_type=F32)[:, 1:2]
    pooled_ref[0] = (sums / jnp.maximum(counts, 1.0)).astype(BF16)

    def drain_pack(r, c):
        for buffers in (tags, pools):
            pack_copy(buffers, lax.rem(pk + r, n_pack), pk).wait_send()
        return c

    lax.fori_loop(1, n_pack, drain_pack, 0)
    store.wait()


def local(queries, keys, values, w_out, norm_gain, block_owner, block_base, frame_offset):
    n_tm = lax.axis_size("tm")
    n_pack = lax.axis_size("pack")
    _, frames, width = queries.shape
    half = frames // 2
    lands = n_tm * LANDMARKS
    slot_rows = CAPACITY * WINDOW
    any_ref = pl.BlockSpec(memory_space=pl.ANY)
    vmem = pl.BlockSpec(memory_space=pltpu.VMEM)
    smem = pl.BlockSpec(memory_space=pltpu.SMEM)
    dma = pltpu.SemaphoreType.DMA
    bf = lambda *shape: pltpu.VMEM(shape, BF16)
    f32 = lambda *shape: pltpu.VMEM(shape, F32)
    return pl.pallas_call(
        functools.partial(body, n_tm, n_pack, min(512, lands)),
        name="landmark_layer",
        out_shape=(
            jax.ShapeDtypeStruct((1, frames, width), BF16),
            jax.ShapeDtypeStruct((1, POOL_DEV, width), BF16),
        ),
        in_specs=[any_ref] * 4 + [vmem, smem, smem, vmem],
        out_specs=(any_ref, vmem),
        scratch_shapes=[
            bf(frames, width),
            bf(frames, width),
            bf(frames, width),
            bf(width, width),
            bf(n_tm, half, LANE),
            bf(n_tm, half, LANE),
            bf(n_tm, LANDMARKS // 2, LANE),
            bf(n_tm, LANDMARKS // 2, LANE),
            bf(n_tm, LANDMARKS // 2, LANE),
            bf(n_tm, LANDMARKS // 2, LANE),
            bf(2, lands, LANE),
            bf(2, lands, LANE),
            f32(frames, lands),
            f32(frames, lands),
            f32(frames, LANE),
            f32(frames, LANE),
            bf(n_tm, half, LANE),
            bf(n_tm, half, LANE),
            bf(frames, width),
            bf(frames, width),
            bf(n_pack * slot_rows, frames),
            bf(n_pack, slot_rows, LANE),
            bf(n_pack, slot_rows, LANE),
            bf(n_pack, slot_rows, width),
            bf(n_pack, slot_rows, width),
            dma((4,)),
        ]
        + [dma((n_tm,))] * 8
        + [dma((n_pack,))] * 4
        + [dma(())],
        compiler_params=pltpu.CompilerParams(
            collective_id=0, has_side_effects=True, vmem_limit_bytes=56 << 20
        ),
        cost_estimate=pl.CostEstimate(
            flops=20_000_000_000, bytes_accessed=8_000_000, transcendentals=36_000_000
        ),
    )(
        queries,
        keys,
        values,
        w_out,
        norm_gain.reshape(1, width),
        block_owner.reshape(1, -1),
        block_base,
        frame_offset[0],
    )


def solution(mesh):
    return jax.shard_map(
        local,
        mesh=mesh,
        in_specs=(
            P("pack", "tm", None),
            P("pack", "tm", None),
            P("pack", "tm", None),
            P(),
            P(),
            P("pack", "tm", None),
            P("pack", "tm"),
            P("pack", "tm", None),
        ),
        out_specs=(P("pack", "tm", None), P("pack", "tm", None)),
        check_vma=False,
    )
```

time: 89.3 us -> 87.6 us (0.981)
  the two profiles are of different devices: /device:TPU:67 before, /device:TPU:5 now
where the time goes in v3:
time: 87.6 us; the launch traced here: 87.5 us
  Pallas kernels  83.8 us (96%)
  local copies, waits for them, and re-layouts  3.01 us (3%)
    pallas_call x1, Pallas kernels, local(): pl.pallas_call(functools.partial(body, n_tm, n_pack, min(512, lands)), na...  83.8 us
    unnamed x4, local copies, waits for them, and re-layouts  3.01 us

profile of v3, /device:TPU:5, one launch (start us, length us, event | category | flops | bytes accessed | tf_op | source)
XLA Modules:
  0.0 87.5 jit_solution(13540765613741022638)
XLA Ops:
  0.6 83.8 %landmark_layer.1 = (bf16[1,512,1024]{2,1,0:T(8,128)(2,1)}, bf16[1,128,1024]{2,1,0:T(8,128)(2,1)}) custom-call(bf16[1,512,1024]{2,1,0:T(8,128)(2,1)} %q_hbm.1, bf16[1,512,1024]{2,1,0:T(8,128)(2,1)} %k_hbm.1, bf16[1,512,1024]{2,1,0:T(8,128)(2,1)} %v_hbm.1, bf16[1024,1024]{1,0:T(8,128)(2,1)} %w_hbm.1, f32[1,1024]{1,0:T(1,128)} %bitcast.3, s32[1,4]{1,0:T(1,128)} %bitcast.5, ...), custom_call_target="tpu_custom_call" | custom-call | flops 20000000000 | bytes 8000000 | tf_op jit(solution)/shard_map/landmark_layer/pallas_call | solution.py:439
  84.4 0.0 copy-start
  84.5 2.3 %copy.12 = bf16[1,512,1024]{2,1,0:T(8,128)(2,1)} copy(bf16[1,512,1024]{2,1,0:T(8,128)(2,1)} %get-tuple-element.4) | data formatting | bytes 2097152
  86.8 0.0 copy-done
  86.8 0.7 copy.13
Async XLA Ops:
  84.4 2.3 %copy-start = (bf16[1,128,1024]{2,1,0:T(8,128)(2,1)S(1)}, bf16[1,128,1024]{2,1,0:T(8,128)(2,1)}, u32[]{:S(2)}) copy-start(bf16[1,128,1024]{2,1,0:T(8,128)(2,1)} %get-tuple-element.5) | copy-start | bytes 786436
